TPU v7x, 512 devices: a whole 4x4x16 slice. The times are simulated.
512 devices in a mesh: col: 64 (over x, z), tm: 8 (over y, core).
Axes of the slice: x: 4, y: 4, z: 16, core: 2. Of those that a mesh axis runs over, the one named last changes fastest.
Arguments:
- series: bfloat16 [1200, 98304], P(None, 'col'), may hold values from -700 to 700
- slab_series: float32 [1200, 2048], P('tm', 'col'), may hold values from -700 to 700
- phase_index: int32 [4, 600], P(None, 'tm'), may hold values from 0 to 1199
Outputs:
- tile_peak: float32 [4, 2048, 64], P(None, None, 'col')
- peak_all: float32 [4], replicated
All inputs are finite; a program needn't handle non-finite values.
Results may differ from a plain program's by a relative error of at most 0.0013.
Values may be sent and summed in bfloat16 or wider, within the bound.
A program may use at most 64 MiB of HBM per device.

v0:
```python
import functools
import math
import jax
import jax.numpy as jnp
from jax import lax
from jax.sharding import Mesh
from jax.sharding import PartitionSpec as P

FRAMES = 1200
FREQS = 600
COL = ("col_0", "col_1")
EPSILON = 1e-06
HIGHEST = lax.Precision.HIGHEST


def laid_out(parts, dim):
    shape = list(parts.shape[1:])
    shape[dim] *= parts.shape[0]
    return jnp.moveaxis(parts, 0, dim).reshape(shape)


def sent_to_all(value, axis):
    copies = jnp.broadcast_to(value, (lax.axis_size(axis), *value.shape))
    return lax.all_to_all(copies, axis, split_axis=0, concat_axis=0, tiled=True)


def gathered_copies(value, axis, dim):
    return laid_out(sent_to_all(value, axis), dim)


def all_blocks(value, axes, sequence):
    parts = value[None]
    for k in sequence:
        parts = lax.all_gather(parts, axes[k], axis=0, tiled=True)
    current = [lax.axis_size(axes[k]) for k in reversed(sequence)]
    parts = parts.reshape(*current, *value.shape)
    turned = sorted(range(len(sequence)), key=lambda place: sequence[len(sequence) - 1 - place])
    return parts.transpose(*turned, *range(len(sequence), parts.ndim)).reshape(-1, *value.shape)


def gathered_by_axis(value, axes, sequence, dim):
    return laid_out(all_blocks(value, axes, sequence), dim)


def by_axis(value, axes):
    return functools.reduce(lax.pmax, axes, value)


def twiddle(frame_ids, freq_ids):
    turn_count = frame_ids[:, None] * freq_ids[None, :] % FRAMES
    angles = turn_count.astype(jnp.float32) * (2.0 * math.pi / FRAMES)
    return (jnp.cos(angles), jnp.sin(angles))


def rotate_back(spec_cos, spec_sin, phase_ids, freq_ids, cos_back, sin_back):
    phase_angle = phase_ids.astype(jnp.float32) * (2.0 * math.pi / FRAMES)
    phase_cos = jnp.cos(phase_angle)[:, :, None]
    phase_sin = jnp.sin(phase_angle)[:, :, None]
    weights = (jnp.where(freq_ids < FREQS, 2.0, 1.0) / FRAMES).astype(jnp.float32)[None, :, None]
    rot_real = (spec_cos[None] * phase_cos + spec_sin[None] * phase_sin) * weights
    rot_imag = (spec_cos[None] * phase_sin - spec_sin[None] * phase_cos) * weights
    return jnp.einsum("sfv,tf->svt", rot_real, cos_back, precision=HIGHEST) - jnp.einsum(
        "sfv,tf->svt", rot_imag, sin_back, precision=HIGHEST
    )


def normalize_rows(surrogate):
    return (
        surrogate * lax.rsqrt(jnp.sum(surrogate * surrogate, axis=2, keepdims=True) + EPSILON)
    ).astype(jnp.bfloat16)


def peak_update(normed_rows, normed_cols):
    scores = jnp.einsum("srt,tc->src", normed_rows, normed_cols, preferred_element_type=jnp.float32)
    row_top = jnp.max(jnp.abs(scores), axis=2)
    return row_top


def body(series, slab_series, phase_index):
    values = series.astype(jnp.float32)
    centered = values - jnp.mean(values, axis=0, keepdims=True)
    normed_cols = (
        centered * lax.rsqrt(jnp.sum(centered * centered, axis=0, keepdims=True) + EPSILON)
    ).astype(jnp.bfloat16)
    surr_count = phase_index.shape[0]
    n_col = lax.axis_size(COL)
    n_tm = lax.axis_size("tm")
    row_share = slab_series.shape[1] // n_tm
    own_frames = lax.all_to_all(slab_series, "tm", split_axis=1, concat_axis=0, tiled=True)
    own_phase = gathered_copies(phase_index, "tm", 1)
    every_freq = jnp.arange(1, FREQS + 1, dtype=jnp.int32)
    cos_every, sin_every = twiddle(jnp.arange(FRAMES, dtype=jnp.int32), every_freq)
    own_cos = jnp.dot(cos_every.T, own_frames, precision=HIGHEST)
    own_sin = jnp.dot(sin_every.T, own_frames, precision=HIGHEST)
    own_normed = normalize_rows(
        rotate_back(own_cos, own_sin, own_phase, every_freq, cos_every, sin_every)
    )
    running = peak_update(gathered_by_axis(own_normed, COL, (0, 1), 1), normed_cols)
    scaled = running * math.sqrt(FRAMES)
    gathered = gathered_copies(scaled.reshape(surr_count, n_col, 1, row_share), "tm", 2)
    full_peaks = gathered.reshape(surr_count, n_col * n_tm * row_share)
    peak_all = by_axis(jnp.max(full_peaks, axis=1), COL)
    return (full_peaks[:, :, None], peak_all)


def solution(mesh):
    finer = Mesh(mesh.devices.reshape(4, 16, mesh.shape["tm"]), ("col_0", "col_1", "tm"))
    placed = (P(None, COL), P("tm", COL), P(None, "tm"))
    return jax.shard_map(
        body, mesh=finer, in_specs=placed, out_specs=(P(None, None, COL), P()), check_vma=False
    )
```

profile of v0, /device:TPU:8, one launch (start us, length us, event | category | flops | bytes accessed | tf_op | source)
XLA Modules:
  0.0 242.8 jit_solution(10669539949304442477)
XLA Ops:
  7.2 1.3 broadcast_in_dim.14
  8.4 9.0 %all-to-all-start.1 = ((s32[8,4,75]{2,1,0:T(4,128)}), s32[8,4,75]{2,1,0:T(4,128)S(1)}, u32[]{:S(2)}, u32[]{:S(2)}) async-start(s32[8,4,75]{2,1,0:T(4,128)} %broadcast_in_dim.14), calls=%async_computation.1 | async-start | bytes 32768 | tf_op jit(solution)/shard_map/all_to_all | solution.py:24
  17.5 1.4 all_to_all.20
  18.9 2.5 %all-to-all-done.1 = s32[8,4,75]{2,1,0:T(4,128)S(1)} async-done(((s32[8,4,75]{2,1,0:T(4,128)}), s32[8,4,75]{2,1,0:T(4,128)S(1)}, u32[]{:S(2)}, u32[]{:S(2)}) %all-to-all-start.1) | async-done | bytes 9632 | tf_op jit(solution)/shard_map/all_to_all | solution.py:24
  21.4 4.7 %all-to-all-start = ((f32[150,8,4]{0,2,1:T(4,128)}), f32[150,8,4]{0,2,1:T(4,128)S(1)}, u32[]{:S(2)}, u32[]{:S(2)}) async-start(f32[150,8,4]{0,2,1:T(4,128)} %all_to_all.20), calls=%async_computation | async-start | bytes 65536 | tf_op jit(solution)/shard_map/all_to_all | solution.py:89
  26.1 0.0 all-gather.3.cloned.1.call-start
  26.1 0.1 cosine_bitcast_fusion
  26.3 0.1 cos.21
  26.3 0.1 sin.21
  26.4 3.7 %all-to-all-done = f32[150,8,4]{0,2,1:T(4,128)S(1)} async-done(((f32[150,8,4]{0,2,1:T(4,128)}), f32[150,8,4]{0,2,1:T(4,128)S(1)}, u32[]{:S(2)}, u32[]{:S(2)}) %all-to-all-start) | async-done | bytes 19232 | tf_op jit(solution)/shard_map/all_to_all | solution.py:89
  30.1 0.1 all_to_all.23
  30.2 14.0 %fusion.19 = f32[600,4]{0,1:T(4,128)S(1)} fusion(f32[1200,4]{0,1:T(4,128)S(1)} %all_to_all.23, s32[600]{0:T(1024)S(1)} %iota_add_fusion), kind=kOutput, calls=%fused_computation.22 | convolution fusion | flops 41040000 | bytes 31200 | tf_op jit(solution)/shard_map/dot_general | solution.py:93
  44.2 14.1 %fusion.22 = f32[600,4]{0,1:T(4,128)S(1)} fusion(f32[1200,4]{0,1:T(4,128)S(1)} %all_to_all.23, s32[600]{0:T(1024)S(1)} %iota_add_fusion), kind=kOutput, calls=%fused_computation.23 | convolution fusion | flops 41040000 | bytes 31200 | tf_op jit(solution)/shard_map/dot_general | solution.py:94
  58.3 15.3 %fusion.10 = f32[4,4,1200]{2,1,0:T(4,128)S(1)} fusion(s32[600]{0:T(1024)S(1)} %iota_add_fusion, f32[600]{0:T(1024)S(1)} %select_multiply_fusion, f32[4,600]{1,0:T(4,128)S(1)} %sin.21, f32[600,4]{0,1:T(4,128)S(1)} %fusion.22, f32[4,600]{1,0:T(4,128)S(1)} %cos.21, f32[600,4]{0,1:T(4,128)S(1)} %fusion.19), kind=kOutput, calls=%fused_computation.13 | convolution fusion | flops 144758400 | bytes 120000 | tf_op jit(solution)/shard_map/sfv,tf->svt/dot_general | solution.py:62
  73.6 15.3 %multiply_reduce_fusion = (f32[4,4]{1,0:T(4,128)S(1)}, f32[4,4,1200]{2,1,0:T(4,128)S(1)}) fusion(f32[4,4,1200]{2,1,0:T(4,128)S(1)} %fusion.10, s32[600]{0:T(1024)S(1)} %iota_add_fusion, f32[600]{0:T(1024)S(1)} %select_multiply_fusion, f32[4,600]{1,0:T(4,128)S(1)} %sin.21, f32[600,4]{0,1:T(4,128)S(1)} %fusion.22, f32[4,600]{1,0:T(4,128)S(1)} %cos.21, ...), kind=kOutput, calls=%fused_computation.40 | convolution fusion | flops 144815984 | bytes 196864 | tf_op jit(solution)/shard_map/sfv,tf->svt/dot_general | solution.py:62
  88.9 0.1 multiply_convert_fusion
  89.0 13.1 %all-gather = bf16[16,4,1200]{2,1,0:T(4,128)(2,1)} all-gather(bf16[4,4,1200]{2,1,0:T(4,128)(2,1)S(1)} %multiply_convert_fusion), channel_id=2, replica_groups=mesh['col_0'=4,'col_1'=16,'tm'=8] {'col_0'}, dimensions={0}, use_global_device_ids=true | all-gather | bytes 192000 | tf_op jit(solution)/shard_map/all_gather | solution.py:34
  102.0 0.0 all-gather.3.cloned.1.call-update
  102.1 0.0 copy-start
  102.1 2.8 %convert_reduce_fusion = f32[1536]{0:T(1024)S(1)} fusion(bf16[1200,1536]{1,0:T(8,128)(2,1)} %param.3), kind=kLoop, calls=%fused_computation.1 | loop fusion | flops 3684864 | bytes 3692544 | tf_op jit(solution)/shard_map/reduce_sum | solution.py:81
  104.9 0.4 copy-done
  105.2 1.0 fusion.2
  106.3 69.0 %all-gather.3.cloned.1.call-done = bf16[64,4,4,1200]{3,2,1,0:T(4,128)(2,1)} async-done(((bf16[4,4,4,1200]{3,2,1,0:T(4,128)(2,1)}), bf16[64,4,4,1200]{3,2,1,0:T(4,128)(2,1)}) %all-gather.3.cloned.1.call-update) | async-done | bytes 2457616 | tf_op jit(solution)/shard_map/all_gather | solution.py:34
  175.3 0.0 copy-start.1
  175.3 3.0 %copy.19 = bf16[4,16,4,4,1200]{4,2,3,1,0:T(4,128)(2,1)S(1)} copy(bf16[4,16,4,4,1200]{4,3,2,0,1:T(4,128)(2,1)} %bitcast.44) | data formatting | bytes 4915200 | tf_op jit(solution)/shard_map/transpose | solution.py:38
  178.2 0.0 copy-done.1
  178.2 4.7 %abs_reduce_fusion = f32[4,256]{1,0:T(4,128)S(1)} fusion(bf16[1200,1536]{1,0:T(8,128)(2,1)S(1)} %copy-done.1, f32[1536]{0:T(1024)S(1)} %add_rsqrt_fusion, f32[1536]{0:T(1024)S(1)} %broadcast_multiply_fusion, bf16[4,256,1200]{2,0,1:T(4,128)(2,1)S(1)} %bitcast.45), kind=kOutput, calls=%fused_computation.6 | convolution fusion | flops 3785391104 | bytes 6160384 | tf_op jit(solution)/shard_map/srt,tc->src/dot_general | solution.py:74
  182.9 0.1 mul.177
  183.1 0.1 copy.21
  183.2 0.1 reshape.75
  183.3 8.6 %all_to_all.29 = f32[8,1,1024]{2,1,0:T(1,128)S(1)} all-to-all(f32[8,1,1024]{2,1,0:T(1,128)S(1)} %reshape.75), channel_id=1, replica_groups=mesh['col_0'=4,'col_1'=16,'tm'=8] {'tm'}, dimensions={0} | all-to-all | bytes 65536 | tf_op jit(solution)/shard_map/all_to_all | solution.py:24
  191.9 0.5 broadcast.66
  192.4 0.7 reduce.2
  193.2 0.1 reshape.76
  193.3 0.1 bitcast_reduce_fusion
  193.4 0.4 copy.22
  193.9 10.4 %pmax.14 = f32[4]{0:T(128)S(1)} all-reduce(f32[4]{0:T(128)S(1)} %bitcast_reduce_fusion), channel_id=1, replica_groups=mesh['col_0'=4,'col_1'=16,'tm'=8] {'col_0'}, use_global_device_ids=true, to_apply=%region_5.6 | all-reduce | flops 4 | bytes 32 | tf_op jit(solution)/shard_map/pmax | solution.py:46
  204.3 1.4 broadcast_in_dim_reshape_reshape.4
  205.6 30.3 %pmax.15 = f32[4]{0:T(128)} all-reduce(f32[4]{0:T(128)S(1)} %pmax.14), channel_id=1, replica_groups=mesh['col_0'=4,'col_1'=16,'tm'=8] {'col_1'}, use_global_device_ids=true, to_apply=%region_6.7 | all-reduce | flops 4 | bytes 32 | tf_op jit(solution)/shard_map/pmax | solution.py:46
  (11 shorter events, 0.1 us)
Async XLA Ops:
  8.4 13.0 %all-to-all-start.1 = ((s32[8,4,75]{2,1,0:T(4,128)}), s32[8,4,75]{2,1,0:T(4,128)S(1)}, u32[]{:S(2)}, u32[]{:S(2)}) async-start(s32[8,4,75]{2,1,0:T(4,128)} %broadcast_in_dim.14), calls=%async_computation.1 | async-start | bytes 32768 | tf_op jit(solution)/shard_map/all_to_all | solution.py:24
  21.4 8.7 %all-to-all-start = ((f32[150,8,4]{0,2,1:T(4,128)}), f32[150,8,4]{0,2,1:T(4,128)S(1)}, u32[]{:S(2)}, u32[]{:S(2)}) async-start(f32[150,8,4]{0,2,1:T(4,128)} %all_to_all.20), calls=%async_computation | async-start | bytes 65536 | tf_op jit(solution)/shard_map/all_to_all | solution.py:89
  26.1 149.2 %all-gather.3.cloned.1.call-start = ((), (), s32[]{:S(2)}) async-start(), calls=%async_computation.3 | async-start | bytes 2785280 | tf_op jit(solution)/shard_map/all_gather | solution.py:34
  102.1 3.2 %copy-start = (bf16[1200,1536]{1,0:T(8,128)(2,1)S(1)}, bf16[1200,1536]{1,0:T(8,128)(2,1)}, u32[]{:S(2)}) copy-start(bf16[1200,1536]{1,0:T(8,128)(2,1)} %param.3) | copy-start | bytes 11059204
  175.3 3.0 %copy-start.1 = (bf16[1200,1536]{1,0:T(8,128)(2,1)S(1)}, bf16[1200,1536]{1,0:T(8,128)(2,1)}, u32[]{:S(2)}) copy-start(bf16[1200,1536]{1,0:T(8,128)(2,1)} %param.3) | copy-start | bytes 11059204
Sparse Core Ops, SparseCore 0:
  102.2 73.0 all-gather.2
where the time goes:
time: 243 us
  waiting for transfers between devices  75.2 us (31%)
  matrix products  63.3 us (26%)
  blocking collectives  62.4 us (26%)
  between operations  14.2 us (6%)
  starting transfers between devices  13.7 us (6%)
  local copies, waits for them, and re-layouts  9.04 us (4%)
  other arithmetic  4.89 us (2%)
    all_gather x1, waiting for transfers between devices, all_blocks(): parts = lax.all_gather(parts, axes[k], axis=0, tiled=True)  69 us
    pmax x2, blocking collectives, by_axis(): return functools.reduce(lax.pmax, axes, value)  40.8 us
    dot_general x1, matrix products, rotate_back(): jnp.einsum('sfv,tf->svt', rot_real, cos_back, precision=HIGHEST)  15.3 us
    dot_general x1, matrix products, rotate_back(): jnp.einsum('sfv,tf->svt', rot_imag, sin_back, precision=HIGHEST)  15.3 us
    dot_general x1, matrix products, body(): own_sin = jnp.dot(sin_every.T, own_frames, precision=HIGHEST)  14.1 us
    dot_general x1, matrix products, body(): own_cos = jnp.dot(cos_every.T, own_frames, precision=HIGHEST)  14 us
    all_gather x1, blocking collectives, all_blocks(): parts = lax.all_gather(parts, axes[k], axis=0, tiled=True)  13.1 us
    all_to_all x1, starting transfers between devices, sent_to_all(): return lax.all_to_all(copies, axis, split_axis=0, concat_axis=0, tiled=True)  9.04 us
  transfers between devices with their start and end apart: 3, of which 3 were waited for; matrix products, arithmetic and copies ran while one was open for 2% of the time, Pallas kernels for 0%

commit v1 on v0

--- a/solution.py
+++ b/solution.py
@@ -11,6 +11,11 @@
 COL = ("col_0", "col_1")
 EPSILON = 1e-06
 HIGHEST = lax.Precision.HIGHEST
+
+
+def gather_over(value, axis, dim):
+    repeated = jnp.stack([value] * lax.axis_size(axis))
+    return jnp.concatenate(lax.all_to_all(repeated, axis, 0, 0), axis=dim)
 
 
 def laid_out(parts, dim):
@@ -31,7 +36,7 @@
 def all_blocks(value, axes, sequence):
     parts = value[None]
     for k in sequence:
-        parts = lax.all_gather(parts, axes[k], axis=0, tiled=True)
+        parts = gather_over(parts, axes[k], 0)
     current = [lax.axis_size(axes[k]) for k in reversed(sequence)]
     parts = parts.reshape(*current, *value.shape)
     turned = sorted(range(len(sequence)), key=lambda place: sequence[len(sequence) - 1 - place])

time: 243 us -> 281 us (1.16)
  the two profiles are of different devices: /device:TPU:8 before, /device:TPU:2 now
where the time goes in v1:
time: 281 us
  waiting for transfers between devices  118 us (42%)
  matrix products  63.5 us (23%)
  blocking collectives  60.6 us (22%)
  starting transfers between devices  20.6 us (7%)
  local copies, waits for them, and re-layouts  12.1 us (4%)
  other arithmetic  4.9 us (2%)
    all_to_all x1, waiting for transfers between devices, gather_over(): return jnp.concatenate(lax.all_to_all(repeated, axis, 0, 0), axis=dim)  109 us
    pmax x2, blocking collectives, by_axis(): return functools.reduce(lax.pmax, axes, value)  41.1 us
    dot_general x1, matrix products, rotate_back(): jnp.einsum('sfv,tf->svt', rot_real, cos_back, precision=HIGHEST)  15.5 us
    dot_general x1, matrix products, rotate_back(): jnp.einsum('sfv,tf->svt', rot_imag, sin_back, precision=HIGHEST)  15.3 us
    dot_general x1, matrix products, body(): own_sin = jnp.dot(sin_every.T, own_frames, precision=HIGHEST)  14.1 us
    dot_general x1, matrix products, body(): own_cos = jnp.dot(cos_every.T, own_frames, precision=HIGHEST)  14 us
    all_to_all x1, starting transfers between devices, gather_over(): return jnp.concatenate(lax.all_to_all(repeated, axis, 0, 0), axis=dim)  12.8 us
    all_to_all x1, blocking collectives, gather_over(): return jnp.concatenate(lax.all_to_all(repeated, axis, 0, 0), axis=dim)  11.7 us
  transfers between devices with their start and end apart: 3, of which 3 were waited for; matrix products, arithmetic and copies ran while one was open for 1% of the time, Pallas kernels for 0%

profile of v1, /device:TPU:2, one launch (start us, length us, event | category | flops | bytes accessed | tf_op | source)
XLA Modules:
  0.0 280.7 jit_solution(9408575678250956931)
XLA Ops:
  0.6 1.3 broadcast_in_dim.12
  1.9 4.5 %all-to-all-start.1 = ((s32[8,4,75]{2,1,0:T(4,128)}), s32[8,4,75]{2,1,0:T(4,128)S(1)}, u32[]{:S(2)}, u32[]{:S(2)}) async-start(s32[8,4,75]{2,1,0:T(4,128)} %broadcast_in_dim.12), calls=%async_computation.1 | async-start | bytes 32768 | tf_op jit(solution)/shard_map/all_to_all | solution.py:29
  6.4 1.4 all_to_all.26
  7.8 4.0 %all-to-all-done.1 = s32[8,4,75]{2,1,0:T(4,128)S(1)} async-done(((s32[8,4,75]{2,1,0:T(4,128)}), s32[8,4,75]{2,1,0:T(4,128)S(1)}, u32[]{:S(2)}, u32[]{:S(2)}) %all-to-all-start.1) | async-done | bytes 9632 | tf_op jit(solution)/shard_map/all_to_all | solution.py:29
  11.7 3.3 %all-to-all-start = ((f32[150,8,4]{0,2,1:T(4,128)}), f32[150,8,4]{0,2,1:T(4,128)S(1)}, u32[]{:S(2)}, u32[]{:S(2)}) async-start(f32[150,8,4]{0,2,1:T(4,128)} %all_to_all.26), calls=%async_computation | async-start | bytes 65536 | tf_op jit(solution)/shard_map/all_to_all | solution.py:94
  15.1 0.1 cosine_bitcast_fusion
  15.2 0.1 cos.21
  15.3 0.1 sin.21
  15.4 5.0 %all-to-all-done = f32[150,8,4]{0,2,1:T(4,128)S(1)} async-done(((f32[150,8,4]{0,2,1:T(4,128)}), f32[150,8,4]{0,2,1:T(4,128)S(1)}, u32[]{:S(2)}, u32[]{:S(2)}) %all-to-all-start) | async-done | bytes 19232 | tf_op jit(solution)/shard_map/all_to_all | solution.py:94
  20.5 0.1 all_to_all.29
  20.6 14.0 %fusion.19 = f32[600,4]{0,1:T(4,128)S(1)} fusion(f32[1200,4]{0,1:T(4,128)S(1)} %all_to_all.29, s32[600]{0:T(1024)S(1)} %iota_add_fusion), kind=kOutput, calls=%fused_computation.22 | convolution fusion | flops 41040000 | bytes 31200 | tf_op jit(solution)/shard_map/dot_general | solution.py:98
  34.6 14.1 %fusion.22 = f32[600,4]{0,1:T(4,128)S(1)} fusion(f32[1200,4]{0,1:T(4,128)S(1)} %all_to_all.29, s32[600]{0:T(1024)S(1)} %iota_add_fusion), kind=kOutput, calls=%fused_computation.23 | convolution fusion | flops 41040000 | bytes 31200 | tf_op jit(solution)/shard_map/dot_general | solution.py:99
  48.7 15.3 %fusion.10 = f32[4,4,1200]{2,1,0:T(4,128)S(1)} fusion(s32[600]{0:T(1024)S(1)} %iota_add_fusion, f32[600]{0:T(1024)S(1)} %select_multiply_fusion, f32[4,600]{1,0:T(4,128)S(1)} %sin.21, f32[600,4]{0,1:T(4,128)S(1)} %fusion.22, f32[4,600]{1,0:T(4,128)S(1)} %cos.21, f32[600,4]{0,1:T(4,128)S(1)} %fusion.19), kind=kOutput, calls=%fused_computation.13 | convolution fusion | flops 144758400 | bytes 120000 | tf_op jit(solution)/shard_map/sfv,tf->svt/dot_general | solution.py:67
  63.9 15.5 %multiply_reduce_fusion = (f32[4,4]{1,0:T(4,128)S(1)}, f32[4,4,1200]{2,1,0:T(4,128)S(1)}) fusion(f32[4,4,1200]{2,1,0:T(4,128)S(1)} %fusion.10, s32[600]{0:T(1024)S(1)} %iota_add_fusion, f32[600]{0:T(1024)S(1)} %select_multiply_fusion, f32[4,600]{1,0:T(4,128)S(1)} %sin.21, f32[600,4]{0,1:T(4,128)S(1)} %fusion.22, f32[4,600]{1,0:T(4,128)S(1)} %cos.21, ...), kind=kOutput, calls=%fused_computation.40 | convolution fusion | flops 144815984 | bytes 196864 | tf_op jit(solution)/shard_map/sfv,tf->svt/dot_general | solution.py:67
  79.4 0.1 multiply_convert_fusion
  79.6 11.7 %all_to_all.39 = bf16[4,1,4,4,1200]{4,2,3,1,0:T(4,128)(2,1)S(1)} all-to-all(bf16[4,1,4,4,1200]{4,2,3,1,0:T(4,128)(2,1)S(1)} %stack.6), channel_id=1, replica_groups=mesh['col_0'=4,'col_1'=16,'tm'=8] {'col_0'}, dimensions={0} | all-to-all | bytes 307200 | tf_op jit(solution)/shard_map/all_to_all | solution.py:18
  91.3 2.5 stack.7
  93.8 12.8 %all-to-all-start.3 = ((bf16[16,4,4,4,1200]{4,2,3,1,0:T(4,128)(2,1)}), bf16[16,4,4,4,1200]{4,2,3,1,0:T(4,128)(2,1)S(1)}, u32[]{:S(2)}, u32[]{:S(2)}) async-start(bf16[16,4,4,4,1200]{4,2,3,1,0:T(4,128)(2,1)} %stack.7), calls=%async_computation.3 | async-start | bytes 5242880 | tf_op jit(solution)/shard_map/all_to_all | solution.py:18
  106.6 0.0 copy-start
  106.6 2.8 convert_reduce_fusion
  109.4 0.4 copy-done
  109.8 1.0 fusion.2
  110.8 109.2 %all-to-all-done.3 = bf16[16,4,4,4,1200]{4,2,3,1,0:T(4,128)(2,1)S(1)} async-done(((bf16[16,4,4,4,1200]{4,2,3,1,0:T(4,128)(2,1)}), bf16[16,4,4,4,1200]{4,2,3,1,0:T(4,128)(2,1)S(1)}, u32[]{:S(2)}, u32[]{:S(2)}) %all-to-all-start.3) | async-done | bytes 2457632 | tf_op jit(solution)/shard_map/all_to_all | solution.py:18
  220.0 1.4 copy.20
  221.4 0.0 copy-start.1
  221.4 2.0 copy.21
  223.4 0.0 copy-done.1
  223.5 4.7 %abs_reduce_fusion = f32[4,256]{1,0:T(4,128)S(1)} fusion(bf16[1200,1536]{1,0:T(8,128)(2,1)S(1)} %copy-done.1, f32[1536]{0:T(1024)S(1)} %add_rsqrt_fusion, f32[1536]{0:T(1024)S(1)} %broadcast_multiply_fusion, bf16[4,256,1200]{2,0,1:T(4,128)(2,1)S(1)} %bitcast.43), kind=kOutput, calls=%fused_computation.6 | convolution fusion | flops 3785391104 | bytes 6160384 | tf_op jit(solution)/shard_map/srt,tc->src/dot_general | solution.py:79
  228.2 0.1 mul.177
  228.3 0.1 copy.23
  228.4 0.1 reshape.74
  228.5 7.8 %all_to_all.40 = f32[8,1,1024]{2,1,0:T(1,128)S(1)} all-to-all(f32[8,1,1024]{2,1,0:T(1,128)S(1)} %reshape.74), channel_id=1, replica_groups=mesh['col_0'=4,'col_1'=16,'tm'=8] {'tm'}, dimensions={0} | all-to-all | bytes 65536 | tf_op jit(solution)/shard_map/all_to_all | solution.py:29
  236.4 0.5 broadcast.69
  236.9 0.7 reduce.2
  237.6 0.1 reshape.75
  237.7 0.1 bitcast_reduce_fusion
  237.8 0.4 copy.24
  238.3 10.6 %pmax.14 = f32[4]{0:T(128)S(1)} all-reduce(f32[4]{0:T(128)S(1)} %bitcast_reduce_fusion), channel_id=1, replica_groups=mesh['col_0'=4,'col_1'=16,'tm'=8] {'col_0'}, use_global_device_ids=true, to_apply=%region_5.6 | all-reduce | flops 4 | bytes 32 | tf_op jit(solution)/shard_map/pmax | solution.py:51
  248.9 1.4 broadcast_in_dim_reshape_reshape.4
  250.3 30.4 %pmax.15 = f32[4]{0:T(128)} all-reduce(f32[4]{0:T(128)S(1)} %pmax.14), channel_id=1, replica_groups=mesh['col_0'=4,'col_1'=16,'tm'=8] {'col_1'}, use_global_device_ids=true, to_apply=%region_6.7 | all-reduce | flops 4 | bytes 32 | tf_op jit(solution)/shard_map/pmax | solution.py:51
  (13 shorter events, 0.1 us)
Async XLA Ops:
  1.9 9.8 %all-to-all-start.1 = ((s32[8,4,75]{2,1,0:T(4,128)}), s32[8,4,75]{2,1,0:T(4,128)S(1)}, u32[]{:S(2)}, u32[]{:S(2)}) async-start(s32[8,4,75]{2,1,0:T(4,128)} %broadcast_in_dim.12), calls=%async_computation.1 | async-start | bytes 32768 | tf_op jit(solution)/shard_map/all_to_all | solution.py:29
  11.7 8.7 %all-to-all-start = ((f32[150,8,4]{0,2,1:T(4,128)}), f32[150,8,4]{0,2,1:T(4,128)S(1)}, u32[]{:S(2)}, u32[]{:S(2)}) async-start(f32[150,8,4]{0,2,1:T(4,128)} %all_to_all.26), calls=%async_computation | async-start | bytes 65536 | tf_op jit(solution)/shard_map/all_to_all | solution.py:94
  93.8 126.1 %all-to-all-start.3 = ((bf16[16,4,4,4,1200]{4,2,3,1,0:T(4,128)(2,1)}), bf16[16,4,4,4,1200]{4,2,3,1,0:T(4,128)(2,1)S(1)}, u32[]{:S(2)}, u32[]{:S(2)}) async-start(bf16[16,4,4,4,1200]{4,2,3,1,0:T(4,128)(2,1)} %stack.7), calls=%async_computation.3 | async-start | bytes 5242880 | tf_op jit(solution)/shard_map/all_to_all | solution.py:18
  106.6 3.2 %copy-start = (bf16[1200,1536]{1,0:T(8,128)(2,1)S(1)}, bf16[1200,1536]{1,0:T(8,128)(2,1)}, u32[]{:S(2)}) copy-start(bf16[1200,1536]{1,0:T(8,128)(2,1)} %param.3) | copy-start | bytes 11059204
  221.4 2.0 copy-start.1
